TPU v7x, 512 devices: a whole 4x4x16 slice. The times are simulated.
512 devices in a mesh: dp: 2 (over z_hi), fsdp: 16 (over z_lo, core), tile: 16 (over y, x).
Axes of the slice: x: 4, y: 4, z: 16 (z_hi: 2, z_lo: 8; z = z_hi * 8 + z_lo), core: 2. Of those that a mesh axis runs over, the one named last changes fastest.
Arguments:
- tokens: bfloat16 [32, 8, 512, 1536], P(('dp', 'fsdp'), None, 'tile'), may hold values from -6 to 6
- norm_gain: float32 [1536], replicated, may hold values from 0.25 to 1.75
- query_key_value_weight: bfloat16 [1536, 2304], P('fsdp'), may hold values from -5 to 5
- out_weight: bfloat16 [768, 1536], P('fsdp'), may hold values from -0.21875 to 0.21875
- head_weight: bfloat16 [1536, 320], P('fsdp'), may hold values from -0.15625 to 0.15625
- coarse: float32 [32, 20, 8, 512], P(('dp', 'fsdp'), None, None, 'tile'), may hold values from -36 to 36
- grad_fine: float32 [32, 20, 32, 2048], P(('dp', 'fsdp'), None, None, 'tile'), may hold values from -0.6 to 0.6
Outputs:
- fine_grid: float32 [32, 20, 32, 2048], P(('dp', 'fsdp'), None, None, 'tile')
- grad_tokens: bfloat16 [32, 8, 512, 1536], P(('dp', 'fsdp'), None, 'tile')
- grad_head: float32 [1536, 320], P('fsdp')
All inputs are finite; a program needn't handle non-finite values.
Results may differ from a plain program's by a relative error of at most 0.0059.
Values may be sent and summed in bfloat16 or wider, within the bound.
No kernel may reach another device: no remote copies, remote signals or barrier semaphores. Data moves between devices by JAX's collectives and lax.ppermute only.
A program may use at most 64 MiB of HBM per device.

v0:
```python
import jax
import jax.numpy as jnp
from jax import lax
from jax.sharding import PartitionSpec as P

D = 1536
HEADS = 8
HEAD_DIM = 96
VARS = 20
MARGIN = 8
INNER = 768
HEAD_OUT = 320
EPSILON = 1e-05


def with_halo(shard, sides, width):
    for axis, dim in sides:
        devices, length = (lax.axis_size(axis), shard.shape[dim])
        up = [(i, (i + 1) % devices) for i in range(devices)]
        down = [(j, i) for i, j in up]
        last = lax.slice_in_dim(shard, length - width, length, axis=dim)
        leading = lax.slice_in_dim(shard, 0, width, axis=dim)
        before = lax.ppermute(last, axis, up)
        after = lax.ppermute(leading, axis, down)
        shard = jnp.concatenate([before, shard, after], axis=dim)
    return shard


def from_behind(value, axis, steps):
    count = lax.axis_size(axis)
    pairs = [(source, (source + steps) % count) for source in range(count)]
    return lax.ppermute(value, axis, pairs)


def layer_norm(values):
    average = jnp.mean(values, axis=-1, keepdims=True)
    centred = values - average
    variance = jnp.mean(centred * centred, axis=-1, keepdims=True)
    inverse_dev = lax.rsqrt(variance + EPSILON)
    return (centred * inverse_dev, inverse_dev)


def norm_backward(grad_normed, standard, inverse_dev, norm_gain):
    grad_standard = grad_normed * norm_gain
    first_mean = jnp.mean(grad_standard, axis=-1, keepdims=True)
    second_mean = jnp.mean(grad_standard * standard, axis=-1, keepdims=True)
    return inverse_dev * (grad_standard - first_mean - standard * second_mean)


def attend_forward(queries, keys_values):
    query_count = queries.shape[0]
    key_count = keys_values.shape[0]
    score_scale = HEAD_DIM ** (-0.5)
    query_heads = queries.reshape(query_count, HEADS, HEAD_DIM)
    key_heads = keys_values[:, :INNER].reshape(key_count, HEADS, HEAD_DIM)
    value_heads = keys_values[:, INNER:].reshape(key_count, HEADS, HEAD_DIM)
    scores = (
        jnp.einsum("qhd,khd->hqk", query_heads, key_heads, preferred_element_type=jnp.float32)
        * score_scale
    )
    biggest = jnp.max(scores, axis=-1, keepdims=True)
    exponent = jnp.exp(scores - biggest)
    softmax_out = exponent / jnp.sum(exponent, axis=-1, keepdims=True)
    softmax_low = softmax_out.astype(jnp.bfloat16)
    attended = jnp.einsum(
        "hqk,khd->qhd", softmax_low, value_heads, preferred_element_type=jnp.float32
    )
    return (attended.astype(jnp.bfloat16).reshape(query_count, INNER), softmax_out)


def attend_backward(softmax_out, queries, keys_values, grad_attended):
    query_count = queries.shape[0]
    key_count = keys_values.shape[0]
    score_scale = HEAD_DIM ** (-0.5)
    query_heads = queries.reshape(query_count, HEADS, HEAD_DIM)
    key_heads = keys_values[:, :INNER].reshape(key_count, HEADS, HEAD_DIM)
    value_heads = keys_values[:, INNER:].reshape(key_count, HEADS, HEAD_DIM)
    grad_heads = grad_attended.reshape(query_count, HEADS, HEAD_DIM)
    softmax_low = softmax_out.astype(jnp.bfloat16)
    grad_values = jnp.einsum(
        "hqk,qhd->khd", softmax_low, grad_heads, preferred_element_type=jnp.float32
    )
    grad_weights = jnp.einsum(
        "qhd,khd->hqk", grad_heads, value_heads, preferred_element_type=jnp.float32
    )
    weighted = jnp.sum(softmax_out * grad_weights, axis=-1, keepdims=True)
    grad_scores = (softmax_out * (grad_weights - weighted)).astype(jnp.bfloat16)
    grad_queries = (
        jnp.einsum("hqk,khd->qhd", grad_scores, key_heads, preferred_element_type=jnp.float32)
        * score_scale
    )
    grad_keys = (
        jnp.einsum("hqk,qhd->khd", grad_scores, query_heads, preferred_element_type=jnp.float32)
        * score_scale
    )
    pair_gradient_rows = jnp.concatenate(
        [grad_keys.reshape(key_count, INNER), grad_values.reshape(key_count, INNER)], axis=1
    )
    return (grad_queries.astype(jnp.bfloat16).reshape(query_count, INNER), pair_gradient_rows)


def interp_weights(fine_index):
    coarse_cell = fine_index // 4
    phase_index = fine_index % 4
    lower_shift = (phase_index < 2).astype(jnp.int32)
    upper_weight = (2 * phase_index - 3 + 8 * lower_shift).astype(jnp.float32) / 8.0
    return (coarse_cell - lower_shift, upper_weight)


def build_matrix(lower_cell, upper_cell, upper_weight, count):
    columns = jnp.arange(count, dtype=jnp.int32)
    lower_part = jnp.where(
        columns[None, :] == lower_cell[:, None], 1.0 - upper_weight[:, None], 0.0
    )
    upper_portion = jnp.where(columns[None, :] == upper_cell[:, None], upper_weight[:, None], 0.0)
    return lower_part + upper_portion


def contract_last(left_side, right_side):
    return lax.dot_general(
        left_side, right_side, (((1,), (1,)), ((), ())), preferred_element_type=jnp.float32
    )


def shards(tokens, norm_gain, query_key_value_weight, out_weight, head_weight, coarse, grad_fine):
    lat_rows = tokens.shape[1]
    lon_cols = tokens.shape[2]
    row_count = lat_rows * lon_cols
    flattened_rows = tokens[0].reshape(row_count, D).astype(jnp.float32)
    standard, inverse_dev = layer_norm(flattened_rows)
    normed = (standard * norm_gain).astype(jnp.bfloat16)
    full_qkv = lax.all_gather(query_key_value_weight, "fsdp", axis=0, tiled=True)
    projected = jnp.dot(normed, full_qkv, preferred_element_type=jnp.float32).astype(jnp.bfloat16)
    queries = projected[:, :INNER]
    pairs_local = projected[:, INNER:]
    margin_pairs = with_halo(
        pairs_local.reshape(lat_rows, lon_cols, 2 * INNER), (("tile", 1),), MARGIN
    )
    keys_values = margin_pairs.reshape(lat_rows * (lon_cols + 2 * MARGIN), 2 * INNER)
    attended, softmax_out = attend_forward(queries, keys_values)
    full_out = lax.all_gather(out_weight, "fsdp", axis=0, tiled=True)
    mixed_out = jnp.dot(attended, full_out, preferred_element_type=jnp.float32)
    hidden = (flattened_rows + mixed_out).astype(jnp.bfloat16)
    full_head = lax.all_gather(head_weight, "fsdp", axis=0, tiled=True)
    head_out = jnp.dot(hidden, full_head, preferred_element_type=jnp.float32)
    fine_head = (
        head_out.reshape(lat_rows, lon_cols, VARS, 4, 4)
        .transpose(2, 0, 3, 1, 4)
        .reshape(VARS, 4 * lat_rows, 4 * lon_cols)
    )
    coarse_padded_grid = with_halo(coarse[0], (("tile", 2),), 1)
    lat_lower, lat_upper_weight = interp_weights(jnp.arange(4 * lat_rows, dtype=jnp.int32))
    latitude_matrix = build_matrix(
        jnp.clip(lat_lower, 0, lat_rows - 1),
        jnp.clip(lat_lower + 1, 0, lat_rows - 1),
        lat_upper_weight,
        lat_rows,
    )
    lon_lower, lon_upper_weight = interp_weights(jnp.arange(4 * lon_cols, dtype=jnp.int32))
    lon_matrix = build_matrix(lon_lower + 1, lon_lower + 2, lon_upper_weight, lon_cols + 2)
    incomplete_grid = jnp.einsum(
        "lj,kji->kli", latitude_matrix, coarse_padded_grid, precision=lax.Precision.HIGHEST
    )
    residual = jnp.einsum(
        "vrb,cb->vrc", incomplete_grid, lon_matrix, precision=lax.Precision.HIGHEST
    )
    fine_grid = fine_head + residual
    grad_rows = (
        grad_fine[0]
        .reshape(VARS, lat_rows, 4, lon_cols, 4)
        .transpose(1, 3, 0, 2, 4)
        .reshape(row_count, HEAD_OUT)
    )
    grad_rows = grad_rows.astype(jnp.bfloat16)
    head_term = lax.dot_general(
        hidden, grad_rows, (((0,), (0,)), ((), ())), preferred_element_type=jnp.float32
    )
    head_block = lax.psum_scatter(head_term, "fsdp", scatter_dimension=0, tiled=True)
    grad_head = lax.psum(head_block, ("dp", "tile"))
    grad_hidden = contract_last(grad_rows, full_head)
    grad_attended = contract_last(grad_hidden.astype(jnp.bfloat16), full_out).astype(jnp.bfloat16)
    grad_queries, pair_gradient_rows = attend_backward(
        softmax_out, queries, keys_values, grad_attended
    )
    pair_gradient_rows = pair_gradient_rows.reshape(lat_rows, lon_cols + 2 * MARGIN, 2 * INNER)
    from_left = from_behind(pair_gradient_rows[:, lon_cols + MARGIN :], "tile", 1)
    from_right = from_behind(pair_gradient_rows[:, :MARGIN], "tile", -1)
    own_cells = pair_gradient_rows[:, MARGIN : MARGIN + lon_cols]
    own_cells = own_cells + jnp.pad(from_left, ((0, 0), (0, lon_cols - MARGIN), (0, 0)))
    own_cells = own_cells + jnp.pad(from_right, ((0, 0), (lon_cols - MARGIN, 0), (0, 0)))
    grad_all = jnp.concatenate(
        [grad_queries, own_cells.reshape(row_count, 2 * INNER).astype(jnp.bfloat16)], axis=1
    )
    grad_normed = contract_last(grad_all, full_qkv)
    grad_input = grad_hidden + norm_backward(grad_normed, standard, inverse_dev, norm_gain)
    grad_tokens = grad_input.astype(jnp.bfloat16).reshape(1, lat_rows, lon_cols, D)
    return (fine_grid[None], grad_tokens, grad_head)


def solution(mesh):
    placed = (
        P(("dp", "fsdp"), None, "tile", None),
        P(),
        P("fsdp", None),
        P("fsdp", None),
        P("fsdp", None),
        P(("dp", "fsdp"), None, None, "tile"),
        P(("dp", "fsdp"), None, None, "tile"),
    )
    return jax.shard_map(
        shards,
        mesh=mesh,
        in_specs=placed,
        out_specs=(
            P(("dp", "fsdp"), None, None, "tile"),
            P(("dp", "fsdp"), None, "tile", None),
            P("fsdp", None),
        ),
        check_vma=False,
    )
```

profile of v0, /device:TPU:2, one launch (start us, length us, event | category | flops | bytes accessed | tf_op | source)
XLA Modules:
  0.0 943.6 jit_solution(4857148850893295786)
XLA Ops:
  8.7 1.7 fusion.56
  10.4 3.4 collective-permute-start.2
  13.8 6.3 collective-permute-start.3
  20.1 1.3 convert_reduce_fusion
  22.5 1.5 copy.23
  24.0 1.1 convert_element_type.125
  25.7 46.6 %all_gather.11 = bf16[1536,320]{1,0:T(8,128)(2,1)S(1)} all-gather(bf16[96,320]{1,0:T(8,128)(2,1)} %param.11), channel_id=1, replica_groups=mesh['dp'=2,'fsdp'=16,'tile'=16] {'fsdp'}, dimensions={0}, use_global_device_ids=true | all-gather | bytes 1044480 | tf_op jit(solution)/shard_map/all_gather | solution.py:144
  72.3 1.6 fusion.59
  73.9 1.2 multiply_convert_fusion.1
  75.7 2.1 convolution_bitcast_fusion.1
  77.8 55.1 %all-gather.3.cloned.1.call-done = bf16[1536,2304]{1,0:T(8,128)(2,1)} async-done(((bf16[96,2304]{1,0:T(8,128)(2,1)}), bf16[1536,2304]{1,0:T(8,128)(2,1)}) %all-gather.3.cloned.1.call-update) | async-done | bytes 7077904 | tf_op jit(solution)/shard_map/all_gather | solution.py:132
  132.9 5.3 convolution_convert_fusion
  140.0 3.2 collective-permute-start
  143.2 2.8 collective-permute-start.1
  146.0 86.6 %all-gather.5.cloned.1.call-done = bf16[768,1536]{1,0:T(8,128)(2,1)} async-done(((bf16[48,1536]{1,0:T(8,128)(2,1)}), bf16[768,1536]{1,0:T(8,128)(2,1)}) %all-gather.5.cloned.1.call-update) | async-done | bytes 2359312 | tf_op jit(solution)/shard_map/all_gather | solution.py:141
  232.6 3.2 convolution_convert_fusion.1
  235.8 1.9 copy.24
  237.8 1.8 slice.50
  239.6 1.9 copy.18
  241.5 1.4 pad_maximum_fusion
  243.9 2.1 copy.29
  246.1 2.1 copy.28
  248.2 4.0 fusion.57
  252.2 2.9 convolution_convert_fusion.2
  256.0 1.3 fusion.58
  257.3 2.0 fusion.60
  259.3 1.4 reshape.187
  260.7 3.0 copy.20
  263.8 3.0 copy.21
  266.8 2.6 convolution_bitcast_fusion
  269.3 1.6 copy.26
  271.0 2.7 concatenate.20
  274.9 3.0 multiply_reduce_fusion
  278.6 1.1 copy-done.1
  280.2 1.7 copy.25
  281.9 1.9 concatenate.19
  285.2 1.5 copy-done.5
  287.6 3.4 collective-permute-start.4
  291.1 2.8 collective-permute-start.5
  295.5 1.1 fusion.11
  296.7 3.5 collective-permute-done.4
  300.2 3.3 collective-permute-done.5
  303.5 1.7 fusion.6
  305.2 6.3 fusion.52
  311.6 73.0 %reduce-scatter.2.cloned.1.call-done = f32[96,320]{1,0:T(8,128)} async-done(((f32[1536,320]{1,0:T(8,128)}), f32[96,320]{1,0:T(8,128)}) %reduce-scatter.2.cloned.1.call-update) | async-done | bytes 122896 | tf_op jit(solution)/shard_map/reduce_scatter | solution.py:178
  384.5 2.9 add_convert_fusion
  387.4 548.1 %all-reduce.4.cloned.1.call-done = f32[96,320]{1,0:T(8,128)} async-done(((f32[96,320]{1,0:T(8,128)}), f32[96,320]{1,0:T(8,128)}) %all-reduce.4.cloned.1.call-update) | async-done | bytes 122896 | tf_op jit(solution)/shard_map/psum | solution.py:179
  935.5 1.6 copy.32
  (85 shorter events, 13.8 us)
Async XLA Ops:
  7.2 14.4 %copy-start = (bf16[1,8,32,1536]{3,2,1,0:T(8,128)(2,1)S(1)}, bf16[1,8,32,1536]{3,2,1,0:T(8,128)(2,1)}, u32[]{:S(2)}) copy-start(bf16[1,8,32,1536]{3,2,1,0:T(8,128)(2,1)} %param.7) | copy-start | bytes 2359300
  7.2 14.8 %copy-start.19 = (f32[1,20,32,128]{3,2,1,0:T(8,128)S(1)}, f32[1,20,32,128]{3,2,1,0:T(8,128)}, u32[]{:S(2)}) copy-start(f32[1,20,32,128]{3,2,1,0:T(8,128)} %param.13) | copy-start | bytes 983044
  7.2 125.7 %all-gather.3.cloned.1.call-start = ((), (), s32[]{:S(2)}) async-start(), calls=%async_computation.1 | async-start | bytes 7520256 | tf_op jit(solution)/shard_map/all_gather | solution.py:132
  7.9 224.7 %all-gather.5.cloned.1.call-start = ((), (), s32[]{:S(2)}) async-start(), calls=%async_computation.2 | async-start | bytes 2506752 | tf_op jit(solution)/shard_map/all_gather | solution.py:141
  8.7 375.8 %reduce-scatter.2.cloned.1.call-start = ((), (), s32[]{:S(2)}) async-start(), calls=%async_computation.3 | async-start | bytes 2506752 | tf_op jit(solution)/shard_map/reduce_scatter | solution.py:178
  10.4 65.2 %collective-permute-start.2 = (f32[20,8,1]{2,1,0:T(8,128)}, f32[20,8,1]{2,1,0:T(8,128)}, u32[]{:S(2)}, u32[]{:S(2)}) collective-permute-start(f32[20,8,1]{2,1,0:T(8,128)} %get-tuple-element.11), channel_id=1, source_target_pairs={{0,1},{1,2},{2,3},{3,4},{4,5},{5,6},{6,7},{7,8},{8,9},{9,10},{10,1... | collective-permute-start | bytes 1928 | tf_op jit(solution)/shard_map/ppermute | solution.py:23
  13.8 61.8 %collective-permute-start.3 = (f32[20,8,1]{2,1,0:T(8,128)}, f32[20,8,1]{2,1,0:T(8,128)}, u32[]{:S(2)}, u32[]{:S(2)}) collective-permute-start(f32[20,8,1]{2,1,0:T(8,128)} %get-tuple-element.12), channel_id=1, source_target_pairs={{1,0},{2,1},{3,2},{4,3},{5,4},{6,5},{7,6},{8,7},{9,8},{10,9},{11,1... | collective-permute-start | bytes 1928 | tf_op jit(solution)/shard_map/ppermute | solution.py:24
  72.3 1.6 copy-start.20
  72.3 3.4 copy-start.15
  138.2 1.8 copy-start.14
  138.2 1.0 copy-start.7
  140.0 101.5 %collective-permute-start = (bf16[8,8,1536]{2,1,0:T(8,128)(2,1)}, bf16[8,8,1536]{2,1,0:T(8,128)(2,1)}, u32[]{:S(2)}, u32[]{:S(2)}) collective-permute-start(bf16[8,8,1536]{2,1,0:T(8,128)(2,1)} %get-tuple-element.9), channel_id=1, source_target_pairs={{0,1},{1,2},{2,3},{3,4},{4,5},{5,6},{6,7},{7,8},{8,9},{9,10},{10,1... | collective-permute-start | bytes 589832 | tf_op jit(solution)/shard_map/ppermute | solution.py:23
  143.2 98.3 %collective-permute-start.1 = (bf16[8,8,1536]{2,1,0:T(8,128)(2,1)}, bf16[8,8,1536]{2,1,0:T(8,128)(2,1)}, u32[]{:S(2)}, u32[]{:S(2)}) collective-permute-start(bf16[8,8,1536]{2,1,0:T(8,128)(2,1)} %get-tuple-element.10), channel_id=1, source_target_pairs={{1,0},{2,1},{3,2},{4,3},{5,4},{6,5},{7,6},{8,7},{9,8},{10,9},{11,1... | collective-permute-start | bytes 589832 | tf_op jit(solution)/shard_map/ppermute | solution.py:24
  252.2 2.9 copy-start.4
  256.0 1.3 copy-start.10
  257.3 2.0 copy-start.12
  273.7 1.1 copy-start.16
  273.7 1.2 copy-start.17
  273.7 661.8 %all-reduce.4.cloned.1.call-start = ((), (), s32[]{:S(2)}) async-start(), calls=%async_computation.4 | async-start | bytes 294912 | tf_op jit(solution)/shard_map/psum | solution.py:179
  274.9 3.0 copy-start.3
  277.9 1.9 copy-start.9
  278.6 1.2 copy-start.1
  283.8 1.3 copy-start.8
  285.0 8.9 copy-start.2
  285.0 8.9 copy-start.6
  285.2 1.5 copy-start.5
  287.6 12.6 %collective-permute-start.4 = (f32[8,8,1536]{2,1,0:T(8,128)}, f32[8,8,1536]{2,1,0:T(8,128)}, u32[]{:S(2)}, u32[]{:S(2)}) collective-permute-start(f32[8,8,1536]{2,1,0:T(8,128)} %get-tuple-element.5), channel_id=1, source_target_pairs={{0,1},{1,2},{2,3},{3,4},{4,5},{5,6},{6,7},{7,8},{8,9},{9,10},{10,1... | collective-permute-start | bytes 1179656 | tf_op jit(solution)/shard_map/ppermute | solution.py:32
  291.0 4.5 copy-start.11
  291.0 4.5 copy-start.13
  291.0 4.5 copy-start.22
  291.0 4.5 copy-start.23
  291.0 4.5 copy-start.24
  291.1 4.5 copy-start.25
  291.1 12.4 %collective-permute-start.5 = (f32[8,8,1536]{2,1,0:T(8,128)}, f32[8,8,1536]{2,1,0:T(8,128)}, u32[]{:S(2)}, u32[]{:S(2)}) collective-permute-start(f32[8,8,1536]{2,1,0:T(8,128)} %get-tuple-element.6), channel_id=1, source_target_pairs={{0,15},{1,0},{2,1},{3,2},{4,3},{5,4},{6,5},{7,6},{8,7},{9,8},{10,9... | collective-permute-start | bytes 1179656 | tf_op jit(solution)/shard_map/ppermute | solution.py:32
  296.7 8.5 copy-start.18
  296.7 8.6 copy-start.21
Sparse Core Ops, SparseCore 0:
  10.1 122.7 all-gather.2
  135.0 97.5 all-gather.4
  273.8 110.6 reduce-scatter.1
  387.3 548.2 all-reduce.3
where the time goes:
time: 945 us; the launch traced here: 944 us
  waiting for transfers between devices  771 us (82%)
  blocking collectives  46.6 us (5%)
  local copies, waits for them, and re-layouts  41.8 us (4%)
  matrix products  37.3 us (4%)
  starting transfers between devices  22.1 us (2%)
  between operations  14.2 us (2%)
  other arithmetic  10.8 us (1%)
    psum x1, waiting for transfers between devices, shards(): grad_head = lax.psum(head_block, ('dp', 'tile'))  548 us
    all_gather x1, waiting for transfers between devices, shards(): full_out = lax.all_gather(out_weight, 'fsdp', axis=0, tiled=True)  86.6 us
    reduce_scatter x1, waiting for transfers between devices, shards(): lax.psum_scatter(head_term, 'fsdp', scatter_dimension=0, tiled=True)  73 us
    all_gather x1, waiting for transfers between devices, shards(): lax.all_gather(query_key_value_weight, 'fsdp', axis=0, tiled=True)  55.1 us
    all_gather x1, blocking collectives, shards(): full_head = lax.all_gather(head_weight, 'fsdp', axis=0, tiled=True)  46.6 us
  transfers between devices with their start and end apart: 10, of which 6 were waited for; matrix products, arithmetic and copies ran while one was open for 5% of the time, Pallas kernels for 0%

commit v1 on v0

--- a/solution.py
+++ b/solution.py
@@ -176,7 +176,7 @@
         hidden, grad_rows, (((0,), (0,)), ((), ())), preferred_element_type=jnp.float32
     )
     head_block = lax.psum_scatter(head_term, "fsdp", scatter_dimension=0, tiled=True)
-    grad_head = lax.psum(head_block, ("dp", "tile"))
+    grad_head = lax.all_gather(head_block, axis_name=("dp", "tile")).sum(axis=0)
     grad_hidden = contract_last(grad_rows, full_head)
     grad_attended = contract_last(grad_hidden.astype(jnp.bfloat16), full_out).astype(jnp.bfloat16)
     grad_queries, pair_gradient_rows = attend_backward(

time: 945 us -> 537 us (0.57)
  the two profiles are of different devices: /device:TPU:2 before, /device:TPU:96 now
where the time goes in v1:
time: 537 us; the launch traced here: 536 us
  waiting for transfers between devices  367 us (68%)
  blocking collectives  49.9 us (9%)
  matrix products  35.7 us (7%)
  local copies, waits for them, and re-layouts  31.5 us (6%)
  starting transfers between devices  26 us (5%)
  between operations  14.3 us (3%)
  other arithmetic  11.4 us (2%)
    reduce_scatter x1, waiting for transfers between devices, shards(): lax.psum_scatter(head_term, 'fsdp', scatter_dimension=0, tiled=True)  110 us
    all_gather x1, waiting for transfers between devices, shards(): lax.all_gather(query_key_value_weight, 'fsdp', axis=0, tiled=True)  92.6 us
    all_gather x1, waiting for transfers between devices, shards(): grad_head = lax.all_gather(head_block, axis_name=('dp', 'tile')).sum(axis=0)  78.6 us
    all_gather x1, waiting for transfers between devices, shards(): full_out = lax.all_gather(out_weight, 'fsdp', axis=0, tiled=True)  66.7 us
    all_gather x1, blocking collectives, shards(): full_head = lax.all_gather(head_weight, 'fsdp', axis=0, tiled=True)  49.9 us
    ppermute x2, starting transfers between devices, with_halo(): after = lax.ppermute(leading, axis, down)  13 us
    ppermute x2, waiting for transfers between devices, from_behind(): return lax.ppermute(value, axis, pairs)  11.9 us
  transfers between devices with their start and end apart: 10, of which 7 were waited for; matrix products, arithmetic and copies ran while one was open for 12% of the time, Pallas kernels for 0%

profile of v1, /device:TPU:96, one launch (start us, length us, event | category | flops | bytes accessed | tf_op | source)
XLA Modules:
  0.0 535.7 jit_solution(3986231864766762101)
XLA Ops:
  8.7 1.3 convert_reduce_fusion
  10.9 92.6 %all-gather.5.cloned.1.call-done = bf16[1536,2304]{1,0:T(8,128)(2,1)} async-done(((bf16[96,2304]{1,0:T(8,128)(2,1)}), bf16[1536,2304]{1,0:T(8,128)(2,1)}) %all-gather.5.cloned.1.call-update) | async-done | bytes 7077904 | tf_op jit(solution)/shard_map/all_gather | solution.py:132
  103.5 5.0 convolution_convert_fusion
  108.6 0.8 fusion.55
  109.4 6.7 %collective-permute-start.1 = (bf16[8,8,1536]{2,1,0:T(8,128)(2,1)}, bf16[8,8,1536]{2,1,0:T(8,128)(2,1)}, u32[]{:S(2)}, u32[]{:S(2)}) collective-permute-start(bf16[8,8,1536]{2,1,0:T(8,128)(2,1)} %get-tuple-element.10), channel_id=1, source_target_pairs={{1,0},{2,1},{3,2},{4,3},{5,4},{6,5},{7,6},{8,7},{9,8},{10,9},{11,1... | collective-permute-start | bytes 589832 | tf_op jit(solution)/shard_map/ppermute | solution.py:24
  116.1 1.9 collective-permute-start
  118.6 1.5 copy.23
  121.2 6.0 %collective-permute-done = bf16[8,8,1536]{2,1,0:T(8,128)(2,1)} collective-permute-done((bf16[8,8,1536]{2,1,0:T(8,128)(2,1)}, bf16[8,8,1536]{2,1,0:T(8,128)(2,1)}, u32[]{:S(2)}, u32[]{:S(2)}) %collective-permute-start) | collective-permute-done | bytes 196640 | tf_op jit(solution)/shard_map/ppermute | solution.py:23
  127.3 1.1 pad_maximum_fusion
  129.1 2.8 fusion.57
  131.9 2.6 convolution_convert_fusion.2
  134.5 66.7 %all-gather.7.cloned.1.call-done = bf16[768,1536]{1,0:T(8,128)(2,1)} async-done(((bf16[48,1536]{1,0:T(8,128)(2,1)}), bf16[768,1536]{1,0:T(8,128)(2,1)}) %all-gather.7.cloned.1.call-update) | async-done | bytes 2359312 | tf_op jit(solution)/shard_map/all_gather | solution.py:141
  201.2 2.5 fusion.4
  203.7 0.9 copy-done.5
  204.6 2.1 fusion.60
  206.7 109.7 %reduce-scatter.2.cloned.1.call-done = f32[96,320]{1,0:T(8,128)} async-done(((f32[1536,320]{1,0:T(8,128)}), f32[96,320]{1,0:T(8,128)}) %reduce-scatter.2.cloned.1.call-update) | async-done | bytes 122896 | tf_op jit(solution)/shard_map/reduce_scatter | solution.py:178
  316.5 6.3 %collective-permute-start.3 = (f32[20,8,1]{2,1,0:T(8,128)S(1)}, f32[20,8,1]{2,1,0:T(8,128)S(1)}, u32[]{:S(2)}, u32[]{:S(2)}) collective-permute-start(f32[20,8,1]{2,1,0:T(8,128)S(1)} %get-tuple-element.12), channel_id=1, source_target_pairs={{1,0},{2,1},{3,2},{4,3},{5,4},{6,5},{7,6},{8,7},{9,8},{10,9},{11,1... | collective-permute-start | bytes 1928 | tf_op jit(solution)/shard_map/ppermute | solution.py:24
  322.9 1.9 collective-permute-start.2
  325.3 49.9 %all_gather.17 = bf16[1536,320]{1,0:T(8,128)(2,1)S(1)} all-gather(bf16[96,320]{1,0:T(8,128)(2,1)S(1)} %copy-done.23), channel_id=1, replica_groups=mesh['dp'=2,'fsdp'=16,'tile'=16] {'fsdp'}, dimensions={0}, use_global_device_ids=true | all-gather | bytes 1044480 | tf_op jit(solution)/shard_map/all_gather | solution.py:144
  375.3 1.7 fusion.59
  377.5 1.2 convolution_bitcast_fusion.1
  378.7 1.6 convolution_convert_fusion.1
  380.3 1.9 copy.24
  382.2 2.4 fusion.58
  384.6 2.4 reshape.187
  387.0 3.1 copy.20
  390.0 3.2 copy.21
  393.3 3.0 multiply_reduce_fusion
  397.0 1.1 copy-done.1
  398.5 1.7 copy.25
  400.2 1.9 concatenate.19
  402.1 3.6 convolution_bitcast_fusion
  405.7 3.0 copy.26
  408.7 2.7 concatenate.20
  411.6 1.1 copy-done.9
  412.8 1.4 copy-done.6
  414.3 0.9 fusion.53
  415.2 7.0 %collective-permute-start.5 = (f32[8,8,1536]{2,1,0:T(8,128)}, f32[8,8,1536]{2,1,0:T(8,128)}, u32[]{:S(2)}, u32[]{:S(2)}) collective-permute-start(f32[8,8,1536]{2,1,0:T(8,128)} %get-tuple-element.6), channel_id=1, source_target_pairs={{0,15},{1,0},{2,1},{3,2},{4,3},{5,4},{6,5},{7,6},{8,7},{9,8},{10,9... | collective-permute-start | bytes 1179656 | tf_op jit(solution)/shard_map/ppermute | solution.py:32
  422.2 2.1 collective-permute-start.4
  424.9 0.9 copy.27
  425.9 1.1 fusion.11
  427.0 4.3 collective-permute-done.5
  431.3 7.6 %collective-permute-done.4 = f32[8,8,1536]{2,1,0:T(8,128)} collective-permute-done((f32[8,8,1536]{2,1,0:T(8,128)}, f32[8,8,1536]{2,1,0:T(8,128)}, u32[]{:S(2)}, u32[]{:S(2)}) %collective-permute-start.4) | collective-permute-done | bytes 393248 | tf_op jit(solution)/shard_map/ppermute | solution.py:32
  438.9 1.7 fusion.6
  440.7 5.2 fusion.52
  445.9 1.5 add_convert_fusion
  447.4 78.6 %all-gather.9.cloned.1.call-done = f32[3072,320]{1,0:T(8,128)} async-done(((f32[96,320]{1,0:T(8,128)}), f32[3072,320]{1,0:T(8,128)}) %all-gather.9.cloned.1.call-update) | async-done | bytes 3932176 | tf_op jit(solution)/shard_map/all_gather | solution.py:179
  525.9 3.3 reduce_sum.69
  (94 shorter events, 8.2 us)
Async XLA Ops:
  7.2 3.0 copy-start
  7.2 3.4 copy-start.24
  7.2 96.3 %all-gather.5.cloned.1.call-start = ((), (), s32[]{:S(2)}) async-start(), calls=%async_computation.1 | async-start | bytes 7520256 | tf_op jit(solution)/shard_map/all_gather | solution.py:132
  7.9 193.3 %all-gather.7.cloned.1.call-start = ((), (), s32[]{:S(2)}) async-start(), calls=%async_computation.2 | async-start | bytes 2506752 | tf_op jit(solution)/shard_map/all_gather | solution.py:141
  8.7 307.7 %reduce-scatter.2.cloned.1.call-start = ((), (), s32[]{:S(2)}) async-start(), calls=%async_computation.3 | async-start | bytes 2506752 | tf_op jit(solution)/shard_map/reduce_scatter | solution.py:178
  108.5 9.5 %copy-start.12 = (bf16[256,2304]{1,0:T(8,128)(2,1)}, bf16[256,2304]{1,0:T(8,128)(2,1)S(1)}, u32[]{:S(2)}) copy-start(bf16[256,2304]{1,0:T(8,128)(2,1)S(1)} %convolution_convert_fusion) | copy-start | bytes 3538948
  108.5 9.5 %copy-start.22 = (f32[1,20,32,128]{3,2,1,0:T(8,128)S(1)}, f32[1,20,32,128]{3,2,1,0:T(8,128)}, u32[]{:S(2)}) copy-start(f32[1,20,32,128]{3,2,1,0:T(8,128)} %param.13) | copy-start | bytes 983044
  109.4 11.9 %collective-permute-start.1 = (bf16[8,8,1536]{2,1,0:T(8,128)(2,1)}, bf16[8,8,1536]{2,1,0:T(8,128)(2,1)}, u32[]{:S(2)}, u32[]{:S(2)}) collective-permute-start(bf16[8,8,1536]{2,1,0:T(8,128)(2,1)} %get-tuple-element.10), channel_id=1, source_target_pairs={{1,0},{2,1},{3,2},{4,3},{5,4},{6,5},{7,6},{8,7},{9,8},{10,9},{11,1... | collective-permute-start | bytes 589832 | tf_op jit(solution)/shard_map/ppermute | solution.py:24
  116.1 11.2 %collective-permute-start = (bf16[8,8,1536]{2,1,0:T(8,128)(2,1)}, bf16[8,8,1536]{2,1,0:T(8,128)(2,1)}, u32[]{:S(2)}, u32[]{:S(2)}) collective-permute-start(bf16[8,8,1536]{2,1,0:T(8,128)(2,1)} %get-tuple-element.9), channel_id=1, source_target_pairs={{0,1},{1,2},{2,3},{3,4},{4,5},{5,6},{6,7},{7,8},{8,9},{9,10},{10,1... | collective-permute-start | bytes 589832 | tf_op jit(solution)/shard_map/ppermute | solution.py:23
  120.0 1.0 slice-start
  120.5 83.2 %copy-start.13 = (bf16[256,320]{0,1:T(8,128)(2,1)}, bf16[256,320]{0,1:T(8,128)(2,1)S(1)}, u32[]{:S(2)}) copy-start(bf16[256,320]{0,1:T(8,128)(2,1)S(1)} %convert_element_type.125) | copy-start | bytes 491524
  121.2 7.9 %copy-start.10 = (bf16[256,768]{0,1:T(8,128)(2,1)}, bf16[256,768]{0,1:T(8,128)(2,1)S(1)}, u32[]{:S(2)}) copy-start(bf16[256,768]{0,1:T(8,128)(2,1)S(1)} %copy.18) | copy-start | bytes 1179652
  128.8 3.2 copy-start.18
  129.1 2.8 copy-start.7
  203.7 0.9 copy-start.5
  206.7 109.8 %copy-start.16 = (f32[1,20,8,32]{3,2,1,0:T(8,128)S(1)}, f32[1,20,8,32]{3,2,1,0:T(8,128)}, u32[]{:S(2)}) copy-start(f32[1,20,8,32]{3,2,1,0:T(8,128)} %param.12) | copy-start | bytes 61444
  206.7 118.7 %copy-start.23 = (bf16[96,320]{1,0:T(8,128)(2,1)S(1)}, bf16[96,320]{1,0:T(8,128)(2,1)}, u32[]{:S(2)}) copy-start(bf16[96,320]{1,0:T(8,128)(2,1)} %param.11) | copy-start | bytes 184324
  206.7 319.3 %all-gather.9.cloned.1.call-start = ((), (), s32[]{:S(2)}) async-start(), calls=%async_computation.4 | async-start | bytes 4866048 | tf_op jit(solution)/shard_map/all_gather | solution.py:179
  316.5 61.0 %collective-permute-start.3 = (f32[20,8,1]{2,1,0:T(8,128)S(1)}, f32[20,8,1]{2,1,0:T(8,128)S(1)}, u32[]{:S(2)}, u32[]{:S(2)}) collective-permute-start(f32[20,8,1]{2,1,0:T(8,128)S(1)} %get-tuple-element.12), channel_id=1, source_target_pairs={{1,0},{2,1},{3,2},{4,3},{5,4},{6,5},{7,6},{8,7},{9,8},{10,9},{11,1... | collective-permute-start | bytes 1928 | tf_op jit(solution)/shard_map/ppermute | solution.py:24
  322.9 54.6 %collective-permute-start.2 = (f32[20,8,1]{2,1,0:T(8,128)S(1)}, f32[20,8,1]{2,1,0:T(8,128)S(1)}, u32[]{:S(2)}, u32[]{:S(2)}) collective-permute-start(f32[20,8,1]{2,1,0:T(8,128)S(1)} %get-tuple-element.11), channel_id=1, source_target_pairs={{0,1},{1,2},{2,3},{3,4},{4,5},{5,6},{6,7},{7,8},{8,9},{9,10},{10,1... | collective-permute-start | bytes 1928 | tf_op jit(solution)/shard_map/ppermute | solution.py:23
  375.2 2.3 copy-start.17
  375.3 3.5 copy-start.4
  390.0 3.2 copy-start.19
  390.0 3.2 copy-start.20
  393.3 3.0 copy-start.3
  396.3 1.9 copy-start.11
  397.0 1.1 copy-start.1
  411.4 1.3 copy-start.9
  412.7 11.6 %copy-start.2 = (bf16[8,256,384]{2,1,0:T(8,128)(2,1)S(1)}, bf16[8,256,384]{2,1,0:T(8,128)(2,1)}, u32[]{:S(2)}) copy-start(bf16[8,256,384]{2,1,0:T(8,128)(2,1)} %copy-done.1) | copy-start | bytes 4718596
  412.7 11.6 %copy-start.8 = (bf16[384,768]{0,1:T(8,128)(2,1)S(1)}, bf16[384,768]{0,1:T(8,128)(2,1)}, u32[]{:S(2)}) copy-start(bf16[384,768]{0,1:T(8,128)(2,1)} %copy-done.7) | copy-start | bytes 1769476
  412.8 1.4 copy-start.6
  415.2 16.1 %collective-permute-start.5 = (f32[8,8,1536]{2,1,0:T(8,128)}, f32[8,8,1536]{2,1,0:T(8,128)}, u32[]{:S(2)}, u32[]{:S(2)}) collective-permute-start(f32[8,8,1536]{2,1,0:T(8,128)} %get-tuple-element.6), channel_id=1, source_target_pairs={{0,15},{1,0},{2,1},{3,2},{4,3},{5,4},{6,5},{7,6},{8,7},{9,8},{10,9... | collective-permute-start | bytes 1179656 | tf_op jit(solution)/shard_map/ppermute | solution.py:32
  422.2 3.7 copy-start.14
  422.2 3.7 copy-start.15
  422.2 3.7 copy-start.26
  422.2 3.7 copy-start.27
  422.2 3.7 copy-start.28
  422.2 3.7 copy-start.29
  422.2 16.7 %collective-permute-start.4 = (f32[8,8,1536]{2,1,0:T(8,128)}, f32[8,8,1536]{2,1,0:T(8,128)}, u32[]{:S(2)}, u32[]{:S(2)}) collective-permute-start(f32[8,8,1536]{2,1,0:T(8,128)} %get-tuple-element.5), channel_id=1, source_target_pairs={{0,1},{1,2},{2,3},{3,4},{4,5},{5,6},{6,7},{7,8},{8,9},{9,10},{10,1... | collective-permute-start | bytes 1179656 | tf_op jit(solution)/shard_map/ppermute | solution.py:32
  427.0 13.6 %copy-start.21 = (bf16[256,768]{1,0:T(8,128)(2,1)S(1)}, bf16[256,768]{1,0:T(8,128)(2,1)}, u32[]{:S(2)}) copy-start(bf16[256,768]{1,0:T(8,128)(2,1)} %copy.27) | copy-start | bytes 1179652
  427.0 13.6 %copy-start.25 = (f32[1536]{0:T(1024)S(1)}, f32[1536]{0:T(1024)}, u32[]{:S(2)}) copy-start(f32[1536]{0:T(1024)} %param.8) | copy-start | bytes 18436
Sparse Core Ops, SparseCore 0:
  10.1 93.3 all-gather.4
  105.6 95.5 all-gather.6
  206.8 109.5 reduce-scatter.1
  320.5 205.3 all-gather.8
